TPU v7x, 32 devices: a whole 2x2x4 slice. The times are simulated.
32 devices in a mesh: parts: 2 (over x), seq: 16 (over z, y, core).
Axes of the slice: x: 2, y: 2, z: 4, core: 2. Of those that a mesh axis runs over, the one named last changes fastest.
Arguments:
- tokens: bfloat16 [131072, 512], P(('parts', 'seq')), parts along dimension 0, may hold values from -6 to 6
- w_value: bfloat16 [512, 512], replicated, may hold values from -0.25 to 0.25
- w_gate: bfloat16 [512, 512], replicated, may hold values from -0.25 to 0.25
- first_block: bfloat16 [256, 256], replicated, may hold values from -0.375 to 0.375
- second_block: bfloat16 [256, 256], replicated, may hold values from -0.375 to 0.375
- third_block: bfloat16 [256, 256], replicated, may hold values from -0.375 to 0.375
- fourth_block: bfloat16 [256, 256], replicated, may hold values from -0.375 to 0.375
- kernel: bfloat16 [512, 256, 256], P('seq'), may hold values from -6 to 6
- skip_gain: float32 [512], replicated, may hold values from 0.25 to 2
- cotangent: bfloat16 [131072, 512], P(('parts', 'seq')), parts along dimension 0, may hold values from -6 to 6
Outputs:
- grad_tokens: bfloat16 [131072, 512], P(('parts', 'seq')), parts along dimension 0
- grad_kernel: bfloat16 [1024, 256, 256], P(('parts', 'seq')), parts along dimension 0
- grad_weights: float32 [4, 512, 512], P('parts'), parts along dimension 0
- grad_skip: float32 [1024], P('parts'), parts along dimension 0
There are 2 independent parts, one for each index of `parts`. A program takes and returns all parts, laid end to end along the dimension named above; an argument that names none is the same for every part. Nothing has to cross between parts.
All inputs are finite; a program needn't handle non-finite values.
Results may differ from a plain program's by a relative error of at most 0.025.
Values may be sent and summed in bfloat16 or wider, within the bound.
A program may use at most 128 MiB of HBM per device.

v0:
```python
import jax
import jax.numpy as jnp
from jax import lax
from jax.sharding import PartitionSpec as P

D = 512
N1 = 256
N2 = 256


def on_device(
    tokens,
    w_value,
    w_gate,
    first_block,
    second_block,
    third_block,
    fourth_block,
    kernel,
    skip_gain,
    cotangent,
):
    f32 = jnp.float32
    bf16 = jnp.bfloat16
    n_devices = lax.axis_size("seq")
    rows_here = N1 // n_devices
    local_rows = tokens.shape[0]
    value = jnp.dot(tokens, w_value, preferred_element_type=f32).astype(bf16)
    gate = jnp.dot(tokens, w_gate, preferred_element_type=f32).astype(bf16)
    cube = value.reshape(rows_here, N2, D)
    section_one = jnp.einsum("abc,pb->cap", cube, first_block, preferred_element_type=f32).astype(
        bf16
    )
    spectrum = jnp.einsum(
        "cap,qa->cqp",
        lax.all_to_all(section_one, "seq", split_axis=0, concat_axis=1, tiled=True),
        second_block,
        preferred_element_type=f32,
    )
    filtered = (spectrum * kernel.astype(f32)).astype(bf16)
    section_three = jnp.einsum(
        "cqp,rq->crp", filtered, third_block, preferred_element_type=f32
    ).astype(bf16)
    split_three = section_three.reshape(section_three.shape[0], n_devices, rows_here, N2)
    conv = jnp.einsum(
        "crp,sp->rsc",
        lax.all_to_all(split_three, "seq", split_axis=1, concat_axis=0, tiled=True)[:, 0],
        fourth_block,
        preferred_element_type=f32,
    )
    mixed = conv.reshape(local_rows, D) + skip_gain * value.astype(f32)
    upstream = cotangent.astype(f32)
    d_mix = (upstream * gate.astype(f32)).astype(bf16)
    d_gate = (upstream * mixed).astype(bf16)
    d_mix_cube = d_mix.reshape(rows_here, N2, D)
    d_three = jnp.einsum(
        "rsc,sp->crp", d_mix_cube, fourth_block, preferred_element_type=f32
    ).astype(bf16)
    d_freq = jnp.einsum(
        "crp,rq->cqp",
        lax.all_to_all(d_three, "seq", split_axis=0, concat_axis=1, tiled=True),
        third_block,
        preferred_element_type=f32,
    )
    grad_kernel = (d_freq * spectrum).astype(bf16)
    d_spec = (d_freq * kernel.astype(f32)).astype(bf16)
    d_one = jnp.einsum("cqp,qa->cap", d_spec, second_block, preferred_element_type=f32).astype(bf16)
    split_one = d_one.reshape(d_one.shape[0], n_devices, rows_here, N2)
    d_cube = jnp.einsum(
        "cap,pb->abc",
        lax.all_to_all(split_one, "seq", split_axis=1, concat_axis=0, tiled=True)[:, 0],
        first_block,
        preferred_element_type=f32,
    )
    d_value = (d_cube.reshape(local_rows, D) + skip_gain * d_mix.astype(f32)).astype(bf16)
    grad_tokens = (
        jnp.dot(d_value, w_value.T, preferred_element_type=f32)
        + jnp.dot(d_gate, w_gate.T, preferred_element_type=f32)
    ).astype(bf16)
    factor = 1.0 / jnp.sqrt(jnp.asarray(N1 * N2, f32))
    value_term = jnp.dot(tokens.T, d_value, preferred_element_type=f32) * factor
    gate_term = jnp.dot(tokens.T, d_gate, preferred_element_type=f32) * factor
    skip_term = jnp.sum(d_mix.astype(f32) * value.astype(f32), axis=0) * factor
    value_total, gate_total, skip_total = (
        lax.psum(value_term.astype(jnp.bfloat16), "seq").astype(jnp.float32),
        lax.psum(gate_term.astype(jnp.bfloat16), "seq").astype(jnp.float32),
        lax.psum(skip_term.astype(jnp.bfloat16), "seq").astype(jnp.float32),
    )
    return (grad_tokens, grad_kernel, jnp.stack([value_total, gate_total]), skip_total)


def solution(mesh):
    in_specs = (
        P(("parts", "seq"), None),
        P(),
        P(),
        P(),
        P(),
        P(),
        P(),
        P("seq", None, None),
        P(),
        P(("parts", "seq"), None),
    )
    out_specs = (
        P(("parts", "seq"), None),
        P(("parts", "seq"), None, None),
        P("parts", None, None),
        P("parts"),
    )
    return jax.shard_map(
        on_device, mesh=mesh, in_specs=in_specs, out_specs=out_specs, check_vma=False
    )
```

profile of v0, /device:TPU:0, one launch (start us, length us, event | category | flops | bytes accessed | tf_op | source)
XLA Modules:
  0.0 597.8 jit_solution(15915618487453710336)
XLA Ops:
  7.2 0.0 copy-start
  7.2 0.0 copy-start.10
  7.2 6.0 %fusion = bf16[4096,512]{1,0:T(8,128)(2,1)S(1)} fusion(bf16[4096,512]{1,0:T(8,128)(2,1)} %param.19, bf16[4096,512]{1,0:T(8,128)(2,1)} %param.10, bf16[512,512]{1,0:T(8,128)(2,1)} %param.12), kind=kOutput, calls=%fused_computation.7 | convolution fusion | flops 2157969408 | bytes 13107200 | tf_op jit(solution)/shard_map/dot_general | solution.py:29
  13.2 0.0 copy-start.5
  13.2 1.9 copy-done.5
  15.2 0.0 copy-done.10
  15.2 1.3 convert_bitcast_fusion.1
  16.5 4.4 copy.60
  20.9 7.5 %all-to-all-start = ((bf16[512,16,256]{2,1,0:T(8,128)(2,1)}), bf16[512,16,256]{2,1,0:T(8,128)(2,1)}, u32[]{:S(2)}, u32[]{:S(2)}) async-start(bf16[512,16,256]{2,1,0:T(8,128)(2,1)} %copy.60), calls=%async_computation | async-start | bytes 8388608 | tf_op jit(solution)/shard_map/all_to_all | solution.py:61
  28.4 0.0 copy-done
  28.4 0.0 copy-start.11
  28.4 4.6 convolution_convert_fusion
  33.0 0.0 copy-start.6
  33.0 2.0 copy-done.6
  35.0 0.0 copy-done.11
  35.0 1.3 convert_bitcast_fusion
  36.3 4.4 copy.70
  40.7 65.3 %all-to-all-done = bf16[512,16,256]{2,1,0:T(8,128)(2,1)} async-done(((bf16[512,16,256]{2,1,0:T(8,128)(2,1)}), bf16[512,16,256]{2,1,0:T(8,128)(2,1)}, u32[]{:S(2)}, u32[]{:S(2)}) %all-to-all-start) | async-done | bytes 4194336 | tf_op jit(solution)/shard_map/all_to_all | solution.py:61
  106.0 19.7 %all-to-all-start.2 = ((bf16[512,16,256]{2,1,0:T(8,128)(2,1)}), bf16[512,16,256]{2,1,0:T(8,128)(2,1)}, u32[]{:S(2)}, u32[]{:S(2)}) async-start(bf16[512,16,256]{2,1,0:T(8,128)(2,1)} %copy.70), calls=%async_computation.2 | async-start | bytes 8388608 | tf_op jit(solution)/shard_map/all_to_all | solution.py:36
  125.7 6.4 %copy.63 = bf16[32,256,256]{1,2,0:T(8,128)(2,1)} copy(bf16[32,256,256]{2,1,0:T(8,128)(2,1)} %param.17) | data formatting | bytes 8388608 | tf_op args[7]
  132.1 4.7 copy.61
  136.8 66.4 %all-to-all-done.2 = bf16[512,16,256]{2,1,0:T(8,128)(2,1)} async-done(((bf16[512,16,256]{2,1,0:T(8,128)(2,1)}), bf16[512,16,256]{2,1,0:T(8,128)(2,1)}, u32[]{:S(2)}, u32[]{:S(2)}) %all-to-all-start.2) | async-done | bytes 4194336 | tf_op jit(solution)/shard_map/all_to_all | solution.py:36
  203.2 2.8 copy.71
  206.0 0.6 copy-done.7
  206.6 0.0 copy-done.8
  206.7 1.3 fusion.30
  208.0 0.0 copy-start.1
  208.0 0.0 copy-done.9
  208.0 0.0 copy-start.2
  208.0 3.3 fusion.8
  211.3 2.2 copy-done.1
  213.6 0.0 copy-done.2
  213.6 1.3 fusion.16
  214.9 2.5 copy.74
  217.3 19.7 %all-to-all-start.3 = ((bf16[32,16,16,256]{3,2,0,1:T(8,128)(2,1)}), bf16[32,16,16,256]{3,2,0,1:T(8,128)(2,1)}, u32[]{:S(2)}, u32[]{:S(2)}) async-start(bf16[32,16,16,256]{3,2,0,1:T(8,128)(2,1)} %copy.74), calls=%async_computation.3 | async-start | bytes 8388608 | tf_op jit(solution)/shard_map/all_to_all | solution.py:47
  237.0 6.0 fusion.13
  243.0 2.3 copy.66
  245.4 69.2 %all-to-all-done.3 = bf16[32,16,16,256]{3,2,0,1:T(8,128)(2,1)} async-done(((bf16[32,16,16,256]{3,2,0,1:T(8,128)(2,1)}), bf16[32,16,16,256]{3,2,0,1:T(8,128)(2,1)}, u32[]{:S(2)}, u32[]{:S(2)}) %all-to-all-start.3) | async-done | bytes 4194336 | tf_op jit(solution)/shard_map/all_to_all | solution.py:47
  314.6 19.7 %all-to-all-start.1 = ((bf16[32,16,16,256]{3,2,0,1:T(8,128)(2,1)}), bf16[32,16,16,256]{3,2,0,1:T(8,128)(2,1)}, u32[]{:S(2)}, u32[]{:S(2)}) async-start(bf16[32,16,16,256]{3,2,0,1:T(8,128)(2,1)} %copy.66), calls=%async_computation.1 | async-start | bytes 8388608 | tf_op jit(solution)/shard_map/all_to_all | solution.py:71
  334.3 0.0 all-reduce.3.cloned.1.call-start
  334.3 6.4 %copy.76 = bf16[32,256,256]{2,1,0:T(8,128)(2,1)} copy(bf16[32,256,256]{1,2,0:T(8,128)(2,1)} %get-tuple-element.25) | data formatting | bytes 8388608
  340.7 3.7 copy.75
  344.4 4.5 fusion.32
  348.9 62.9 %all-to-all-done.1 = bf16[32,16,16,256]{3,2,0,1:T(8,128)(2,1)} async-done(((bf16[32,16,16,256]{3,2,0,1:T(8,128)(2,1)}), bf16[32,16,16,256]{3,2,0,1:T(8,128)(2,1)}, u32[]{:S(2)}, u32[]{:S(2)}) %all-to-all-start.1) | async-done | bytes 4194336 | tf_op jit(solution)/shard_map/all_to_all | solution.py:71
  411.8 3.8 copy.67
  415.6 0.0 slice-start.1
  415.6 0.0 copy-start.13
  415.7 4.5 fusion.24
  420.2 0.0 slice-done
  420.2 0.0 slice-done.1
  420.2 0.0 copy-done.13
  420.2 10.9 %fusion.7 = (f32[512]{0:T(512)S(1)}, bf16[4096,512]{1,0:T(8,128)(2,1)}, bf16[4096,512]{1,0:T(8,128)(2,1)S(1)}) fusion(bf16[4096,512]{1,0:T(8,128)(2,1)} %copy-done.6, bf16[4096,512]{1,0:T(8,128)(2,1)} %copy-done.5, f32[512]{0:T(512)S(1)} %copy-done.13, f32[512,16,256]{0,2,1:T(8,128)} %fusion.24, f32[512,16,256]{0,2,1:T(8,128)S(1)} %bitcast.101, ...), kind=kLoop, calls=%fused_computation.14 | loop fusion | flops 25165312 | bytes 37752832 | tf_op jit(solution)/shard_map/reduce_sum | solution.py:83
  431.0 8.2 %fusion.22 = bf16[1,512,512]{1,2,0:T(8,128)(2,1)} fusion(bf16[4096,512]{1,0:T(8,128)(2,1)} %get-tuple-element.23, bf16[4096,512]{1,0:T(8,128)(2,1)} %param.10), kind=kOutput, calls=%fused_computation.31 | convolution fusion | flops 2148007936 | bytes 8912896 | tf_op jit(solution)/shard_map/dot_general | solution.py:81
  439.2 0.0 copy-done.4
  439.2 5.9 fusion.35
  445.1 0.0 copy-done.3
  445.1 3.2 fusion.21
  448.3 47.8 %psum.23 = bf16[512]{0:T(512)(128)(2,1)S(1)} all-reduce(bf16[512]{0:T(512)(128)(2,1)S(1)} %multiply_convert_fusion), channel_id=1, replica_groups=mesh['parts'=2,'seq'=16] {'seq'}, use_global_device_ids=true, to_apply=%region_3.0 | all-reduce | flops 512 | bytes 2048 | tf_op jit(solution)/shard_map/psum | solution.py:87
  496.0 0.6 convert_element_type.116
  496.6 0.0 all-reduce.3.cloned.1.call-update
  496.6 9.2 %add_convert_fusion = bf16[4096,512]{1,0:T(8,128)(2,1)} fusion(f32[4096,512]{1,0:T(8,128)} %fusion.35, bf16[4096,512]{1,0:T(8,128)(2,1)} %copy-done.3, bf16[512,512]{1,0:T(8,128)(2,1)S(1)} %copy-done.12), kind=kOutput, calls=%fused_computation.17 | convolution fusion | flops 2151677952 | bytes 17301504 | tf_op jit(solution)/shard_map/dot_general | solution.py:78
  505.8 82.0 %all-reduce.3.cloned.1.call-done = (bf16[1,512,512]{1,2,0:T(8,128)(2,1)}, bf16[1,512,512]{1,2,0:T(8,128)(2,1)}) async-done(((bf16[1,512,512]{1,2,0:T(8,128)(2,1)}, bf16[1,512,512]{1,2,0:T(8,128)(2,1)}), (bf16[1,512,512]{1,2,0:T(8,128)(2,1)}, bf16[1,512,512]{1,2,0:T(8,128)(2,1)})) %all-reduce.3.cloned.1.call-update) | async-done | bytes 1048592 | tf_op jit(solution)/shard_map/psum | solution.py:86
  587.8 1.3 maximum_convert_fusion
  589.1 1.8 copy.77
  (12 shorter events, 0.0 us)
Async XLA Ops:
  7.2 21.3 %copy-start = (bf16[512,512]{1,0:T(8,128)(2,1)S(1)}, bf16[512,512]{1,0:T(8,128)(2,1)}, u32[]{:S(2)}) copy-start(bf16[512,512]{1,0:T(8,128)(2,1)} %param.11) | copy-start | bytes 1572868
  7.2 8.0 %copy-start.10 = (bf16[256,256]{1,0:T(8,128)(2,1)S(1)}, bf16[256,256]{1,0:T(8,128)(2,1)}, u32[]{:S(2)}) copy-start(bf16[256,256]{1,0:T(8,128)(2,1)} %param.16) | copy-start | bytes 393220
  13.2 1.9 copy-start.5
  20.9 85.0 %all-to-all-start = ((bf16[512,16,256]{2,1,0:T(8,128)(2,1)}), bf16[512,16,256]{2,1,0:T(8,128)(2,1)}, u32[]{:S(2)}, u32[]{:S(2)}) async-start(bf16[512,16,256]{2,1,0:T(8,128)(2,1)} %copy.60), calls=%async_computation | async-start | bytes 8388608 | tf_op jit(solution)/shard_map/all_to_all | solution.py:61
  28.4 6.6 %copy-start.11 = (bf16[256,256]{1,0:T(8,128)(2,1)S(1)}, bf16[256,256]{1,0:T(8,128)(2,1)}, u32[]{:S(2)}) copy-start(bf16[256,256]{1,0:T(8,128)(2,1)} %param.13) | copy-start | bytes 393220
  33.0 2.0 copy-start.6
  106.0 97.2 %all-to-all-start.2 = ((bf16[512,16,256]{2,1,0:T(8,128)(2,1)}), bf16[512,16,256]{2,1,0:T(8,128)(2,1)}, u32[]{:S(2)}, u32[]{:S(2)}) async-start(bf16[512,16,256]{2,1,0:T(8,128)(2,1)} %copy.70), calls=%async_computation.2 | async-start | bytes 8388608 | tf_op jit(solution)/shard_map/all_to_all | solution.py:36
  203.2 3.4 copy-start.7
  203.2 3.5 copy-start.8
  206.6 1.3 copy-start.9
  208.0 5.6 copy-start.1
  208.0 5.6 copy-start.2
  217.3 97.3 %all-to-all-start.3 = ((bf16[32,16,16,256]{3,2,0,1:T(8,128)(2,1)}), bf16[32,16,16,256]{3,2,0,1:T(8,128)(2,1)}, u32[]{:S(2)}, u32[]{:S(2)}) async-start(bf16[32,16,16,256]{3,2,0,1:T(8,128)(2,1)} %copy.74), calls=%async_computation.3 | async-start | bytes 8388608 | tf_op jit(solution)/shard_map/all_to_all | solution.py:47
  314.6 97.2 %all-to-all-start.1 = ((bf16[32,16,16,256]{3,2,0,1:T(8,128)(2,1)}), bf16[32,16,16,256]{3,2,0,1:T(8,128)(2,1)}, u32[]{:S(2)}, u32[]{:S(2)}) async-start(bf16[32,16,16,256]{3,2,0,1:T(8,128)(2,1)} %copy.66), calls=%async_computation.1 | async-start | bytes 8388608 | tf_op jit(solution)/shard_map/all_to_all | solution.py:71
  334.3 253.5 %all-reduce.3.cloned.1.call-start = ((), (), s32[]{:S(2)}) async-start(), calls=%async_computation.4 | async-start | bytes 2097152 | tf_op jit(solution)/shard_map/psum | solution.py:86
  411.8 8.3 %slice-start = ((s8[8388608]{0:T(1024)(128)(4,1)}), s8[4194304]{0:T(1024)(128)(4,1)S(1)}, s32[]{:S(2)}) async-start(s8[8388608]{0:T(1024)(128)(4,1)} %bitcast.100), calls=%async_computation.5 | async-start | bytes 8388608
  415.6 4.5 slice-start.1
  415.6 4.5 copy-start.13
  431.0 14.1 %copy-start.3 = (bf16[4096,512]{1,0:T(8,128)(2,1)}, bf16[4096,512]{1,0:T(8,128)(2,1)S(1)}, u32[]{:S(2)}) copy-start(bf16[4096,512]{1,0:T(8,128)(2,1)S(1)} %get-tuple-element.24) | copy-start | bytes 12582916
  431.0 8.2 %copy-start.4 = (bf16[4096,512]{1,0:T(8,128)(2,1)S(1)}, bf16[4096,512]{1,0:T(8,128)(2,1)}, u32[]{:S(2)}) copy-start(bf16[4096,512]{1,0:T(8,128)(2,1)} %get-tuple-element.23) | copy-start | bytes 12582916
  439.2 5.9 copy-start.14
  445.1 51.5 %copy-start.12 = (bf16[512,512]{1,0:T(8,128)(2,1)S(1)}, bf16[512,512]{1,0:T(8,128)(2,1)}, u32[]{:S(2)}) copy-start(bf16[512,512]{1,0:T(8,128)(2,1)} %param.12) | copy-start | bytes 1572868
Sparse Core Ops, SparseCore 0:
  496.8 90.9 all-reduce.2
where the time goes:
time: 599 us; the launch traced here: 598 us
  waiting for transfers between devices  346 us (58%)
  starting transfers between devices  66.6 us (11%)
  matrix products  60.6 us (10%)
  local copies, waits for them, and re-layouts  50.1 us (8%)
  blocking collectives  47.8 us (8%)
  between operations  14.3 us (2%)
  other arithmetic  12.8 us (2%)
    psum x1, waiting for transfers between devices, on_device(): lax.psum(gate_term.astype(jnp.bfloat16), 'seq').astype(jnp.float32)  82 us
    all_to_all x1, waiting for transfers between devices, on_device(): lax.all_to_all(split_three, 'seq', split_axis=1, concat_axis=0, tiled=True)  69.2 us
    all_to_all x1, waiting for transfers between devices, on_device(): lax.all_to_all(section_one, 'seq', split_axis=0, concat_axis=1, tiled=True)  66.4 us
    all_to_all x1, waiting for transfers between devices, on_device(): lax.all_to_all(d_three, 'seq', split_axis=0, concat_axis=1, tiled=True)  65.3 us
    all_to_all x1, waiting for transfers between devices, on_device(): lax.all_to_all(split_one, 'seq', split_axis=1, concat_axis=0, tiled=True)  62.9 us
    psum x1, blocking collectives, on_device(): lax.psum(skip_term.astype(jnp.bfloat16), 'seq').astype(jnp.float32)  47.8 us
    unnamed x37, local copies, waits for them, and re-layouts  21.5 us
    all_to_all x1, starting transfers between devices, on_device(): lax.all_to_all(split_three, 'seq', split_axis=1, concat_axis=0, tiled=True)  19.7 us
  transfers between devices with their start and end apart: 5, of which 5 were waited for; matrix products, arithmetic and copies ran while one was open for 9% of the time, Pallas kernels for 0%

commit v1 on v0

--- a/solution.py
+++ b/solution.py
@@ -6,6 +6,13 @@
 D = 512
 N1 = 256
 N2 = 256
+
+
+def exchange_blocks(x, axis, split, join):
+    n_dev = lax.axis_size(axis)
+    tiles = jnp.stack(jnp.split(x, n_dev, axis=split), axis=0)
+    tiles = lax.all_to_all(tiles, axis, split_axis=0, concat_axis=0)
+    return jnp.concatenate(tiles, axis=join)
 
 
 def on_device(
@@ -68,7 +75,7 @@
     split_one = d_one.reshape(d_one.shape[0], n_devices, rows_here, N2)
     d_cube = jnp.einsum(
         "cap,pb->abc",
-        lax.all_to_all(split_one, "seq", split_axis=1, concat_axis=0, tiled=True)[:, 0],
+        exchange_blocks(split_one, "seq", 1, 0)[:, 0],
         first_block,
         preferred_element_type=f32,
     )

time: 599 us -> 582 us (0.972)
  waiting for transfers between devices: 346 us -> 325 us
  local copies, waits for them, and re-layouts: 50.1 us -> 57.1 us
    all_to_all x1, waiting for transfers between devices: 66.4 us -> 51.2 us  [on_device(): lax.all_to_all(section_one, 'seq', split_axis=0, concat_axis=1, tiled=True)]
    unnamed x37 -> x42, local copies, waits for them, and re-layouts: 21.5 us -> 32.3 us
    all_to_all x1, waiting for transfers between devices: 69.2 us -> 62.7 us  [on_device(): lax.all_to_all(split_three, 'seq', split_axis=1, concat_axis=0, tiled=True)]
  transfers between devices with their start and end apart: 5 -> 5, of which waited for: 5 -> 5; matrix products, arithmetic and copies ran while one was open for 9% -> 12% of each run, Pallas kernels for 0% -> 0%
where the time goes in v1:
time: 582 us; the launch traced here: 581 us
  waiting for transfers between devices  325 us (56%)
  starting transfers between devices  66.8 us (11%)
  local copies, waits for them, and re-layouts  57.1 us (10%)
  matrix products  56.6 us (10%)
  blocking collectives  48 us (8%)
  between operations  14.3 us (2%)
  other arithmetic  12.9 us (2%)
    psum x1, waiting for transfers between devices, on_device(): lax.psum(gate_term.astype(jnp.bfloat16), 'seq').astype(jnp.float32)  82 us
    all_to_all x1, waiting for transfers between devices, on_device(): lax.all_to_all(d_three, 'seq', split_axis=0, concat_axis=1, tiled=True)  65.2 us
    all_to_all x1, waiting for transfers between devices, exchange_blocks(): tiles = lax.all_to_all(tiles, axis, split_axis=0, concat_axis=0)  64.3 us
    all_to_all x1, waiting for transfers between devices, on_device(): lax.all_to_all(split_three, 'seq', split_axis=1, concat_axis=0, tiled=True)  62.7 us
    all_to_all x1, waiting for transfers between devices, on_device(): lax.all_to_all(section_one, 'seq', split_axis=0, concat_axis=1, tiled=True)  51.2 us
    psum x1, blocking collectives, on_device(): lax.psum(skip_term.astype(jnp.bfloat16), 'seq').astype(jnp.float32)  48 us
    unnamed x42, local copies, waits for them, and re-layouts  32.3 us
    all_to_all x1, starting transfers between devices, on_device(): lax.all_to_all(section_one, 'seq', split_axis=0, concat_axis=1, tiled=True)  19.7 us
  transfers between devices with their start and end apart: 5, of which 5 were waited for; matrix products, arithmetic and copies ran while one was open for 12% of the time, Pallas kernels for 0%

profile of v1, /device:TPU:0, one launch (start us, length us, event | category | flops | bytes accessed | tf_op | source)
XLA Modules:
  0.0 581.1 jit_solution(18249086286279025760)
XLA Ops:
  7.2 0.0 copy-start
  7.2 6.0 %fusion = bf16[4096,512]{1,0:T(8,128)(2,1)S(1)} fusion(bf16[4096,512]{1,0:T(8,128)(2,1)} %param.19, bf16[4096,512]{1,0:T(8,128)(2,1)} %param.10, bf16[512,512]{1,0:T(8,128)(2,1)} %param.12), kind=kOutput, calls=%fused_computation.7 | convolution fusion | flops 2157969408 | bytes 13107200 | tf_op jit(solution)/shard_map/dot_general | solution.py:36
  13.2 1.9 copy-done.4
  15.2 1.3 convert_bitcast_fusion.1
  16.5 4.4 copy.104
  20.9 7.5 %all-to-all-start = ((bf16[512,16,256]{2,1,0:T(8,128)(2,1)}), bf16[512,16,256]{2,1,0:T(8,128)(2,1)}, u32[]{:S(2)}, u32[]{:S(2)}) async-start(bf16[512,16,256]{2,1,0:T(8,128)(2,1)} %copy.104), calls=%async_computation | async-start | bytes 8388608 | tf_op jit(solution)/shard_map/all_to_all | solution.py:68
  28.4 0.0 copy-start.8
  28.5 4.6 convolution_convert_fusion
  33.0 0.0 copy-start.5
  33.0 2.0 copy-done.5
  35.0 1.3 convert_bitcast_fusion
  36.4 4.4 copy.128
  40.8 65.2 %all-to-all-done = bf16[512,16,256]{2,1,0:T(8,128)(2,1)} async-done(((bf16[512,16,256]{2,1,0:T(8,128)(2,1)}), bf16[512,16,256]{2,1,0:T(8,128)(2,1)}, u32[]{:S(2)}, u32[]{:S(2)}) %all-to-all-start) | async-done | bytes 4194336 | tf_op jit(solution)/shard_map/all_to_all | solution.py:68
  106.0 19.7 %all-to-all-start.2 = ((bf16[512,16,256]{2,1,0:T(8,128)(2,1)}), bf16[512,16,256]{2,1,0:T(8,128)(2,1)}, u32[]{:S(2)}, u32[]{:S(2)}) async-start(bf16[512,16,256]{2,1,0:T(8,128)(2,1)} %copy.128), calls=%async_computation.2 | async-start | bytes 8388608 | tf_op jit(solution)/shard_map/all_to_all | solution.py:43
  125.7 6.4 %copy.107 = bf16[32,256,256]{1,2,0:T(8,128)(2,1)} copy(bf16[32,256,256]{2,1,0:T(8,128)(2,1)} %param.17) | data formatting | bytes 8388608 | tf_op args[7]
  132.1 2.8 copy.105
  134.9 0.0 copy-start.6
  134.9 1.3 fusion.46
  136.2 0.8 copy-done.2
  137.1 1.4 fusion.13
  138.5 1.8 copy-done.1
  140.3 0.7 fusion.38
  141.0 0.7 fusion.37
  141.7 0.7 fusion.36
  142.5 0.7 fusion.35
  143.2 0.8 fusion.34
  144.0 0.7 fusion.33
  144.7 0.7 fusion.32
  145.4 0.7 fusion.31
  146.1 0.7 fusion.30
  146.9 0.7 fusion.29
  147.6 0.7 fusion.28
  148.4 0.7 fusion.27
  149.1 0.7 fusion.26
  149.8 0.7 fusion.25
  150.5 0.8 fusion.24
  151.3 0.7 fusion.23
  152.0 51.2 %all-to-all-done.2 = bf16[512,16,256]{2,1,0:T(8,128)(2,1)} async-done(((bf16[512,16,256]{2,1,0:T(8,128)(2,1)}), bf16[512,16,256]{2,1,0:T(8,128)(2,1)}, u32[]{:S(2)}, u32[]{:S(2)}) %all-to-all-start.2) | async-done | bytes 4194336 | tf_op jit(solution)/shard_map/all_to_all | solution.py:43
  203.2 19.7 %all-to-all-start.1 = ((bf16[16,32,1,16,256]{4,3,1,2,0:T(8,128)(2,1)}), bf16[16,32,1,16,256]{4,3,1,2,0:T(8,128)(2,1)}, u32[]{:S(2)}, u32[]{:S(2)}) async-start(bf16[16,32,1,16,256]{4,3,1,2,0:T(8,128)(2,1)} %fusion.23), calls=%async_computation.1 | async-start | bytes 8388608 | tf_op jit(solution)/shard_map/all_to_all | solution.py:14
  222.9 2.7 copy.129
  225.7 6.8 %fusion.8 = (bf16[32,256,256]{1,2,0:T(8,128)(2,1)}, f32[32,256,256]{2,1,0:T(8,128)S(1)}) fusion(f32[32,256,256]{2,1,0:T(8,128)} %copy-done.1, bf16[32,256,256]{2,1,0:T(8,128)(2,1)S(1)} %bitcast.212, bf16[256,256]{1,0:T(8,128)(2,1)S(1)} %copy-done.6), kind=kOutput, calls=%fused_computation.16 | convolution fusion | flops 1077936128 | bytes 25296896 | tf_op jit(solution)/shard_map/cap,qa->cqp/dot_general | solution.py:41
  232.5 1.3 fusion.16
  233.8 2.4 copy.132
  236.2 64.3 %all-to-all-done.1 = bf16[16,32,1,16,256]{4,3,1,2,0:T(8,128)(2,1)} async-done(((bf16[16,32,1,16,256]{4,3,1,2,0:T(8,128)(2,1)}), bf16[16,32,1,16,256]{4,3,1,2,0:T(8,128)(2,1)}, u32[]{:S(2)}, u32[]{:S(2)}) %all-to-all-start.1) | async-done | bytes 4194336 | tf_op jit(solution)/shard_map/all_to_all | solution.py:14
  300.5 19.7 %all-to-all-start.3 = ((bf16[32,16,16,256]{3,2,0,1:T(8,128)(2,1)}), bf16[32,16,16,256]{3,2,0,1:T(8,128)(2,1)}, u32[]{:S(2)}, u32[]{:S(2)}) async-start(bf16[32,16,16,256]{3,2,0,1:T(8,128)(2,1)} %copy.132), calls=%async_computation.3 | async-start | bytes 8388608 | tf_op jit(solution)/shard_map/all_to_all | solution.py:54
  320.2 0.3 all-reduce.3.cloned.1.call-start
  320.4 6.4 %copy.134 = bf16[32,256,256]{2,1,0:T(8,128)(2,1)} copy(bf16[32,256,256]{1,2,0:T(8,128)(2,1)} %get-tuple-element.25) | data formatting | bytes 8388608
  326.8 3.7 copy.125
  330.5 4.5 fusion.40
  335.0 62.7 %all-to-all-done.3 = bf16[32,16,16,256]{3,2,0,1:T(8,128)(2,1)} async-done(((bf16[32,16,16,256]{3,2,0,1:T(8,128)(2,1)}), bf16[32,16,16,256]{3,2,0,1:T(8,128)(2,1)}, u32[]{:S(2)}, u32[]{:S(2)}) %all-to-all-start.3) | async-done | bytes 4194336 | tf_op jit(solution)/shard_map/all_to_all | solution.py:54
  397.7 3.7 copy.133
  401.4 0.0 copy-start.11
  401.4 1.3 fusion.48
  402.7 10.9 %fusion.7 = (f32[512]{0:T(512)S(1)}, bf16[4096,512]{1,0:T(8,128)(2,1)S(1)}, bf16[4096,512]{1,0:T(8,128)(2,1)}) fusion(bf16[4096,512]{1,0:T(8,128)(2,1)} %copy-done.5, bf16[4096,512]{1,0:T(8,128)(2,1)} %copy-done.4, f32[512]{0:T(512)S(1)} %copy-done.11, f32[512,16,256]{0,2,1:T(8,128)} %fusion.40, f32[512,16,256]{0,2,1:T(8,128)S(1)} %fusion.48, ...), kind=kLoop, calls=%fused_computation.14 | loop fusion | flops 25165312 | bytes 37752832 | tf_op jit(solution)/shard_map/reduce_sum | solution.py:90
  413.6 5.3 fusion.22
  419.0 5.6 fusion.51
  424.6 48.0 %psum.23 = bf16[512]{0:T(512)(128)(2,1)S(1)} all-reduce(bf16[512]{0:T(512)(128)(2,1)S(1)} %multiply_convert_fusion), channel_id=1, replica_groups=mesh['parts'=2,'seq'=16] {'seq'}, use_global_device_ids=true, to_apply=%region_3.0 | all-reduce | flops 512 | bytes 2048 | tf_op jit(solution)/shard_map/psum | solution.py:94
  472.6 0.6 convert_element_type.116
  473.2 6.7 %fusion.21 = bf16[1,512,512]{1,2,0:T(8,128)(2,1)} fusion(bf16[4096,512]{1,0:T(8,128)(2,1)} %get-tuple-element.24, bf16[4096,512]{1,0:T(8,128)(2,1)} %param.10), kind=kOutput, calls=%fused_computation.30 | convolution fusion | flops 2148007936 | bytes 8912896 | tf_op jit(solution)/shard_map/dot_general | solution.py:89
  479.9 0.0 all-reduce.3.cloned.1.call-update
  479.9 9.2 %add_convert_fusion = bf16[4096,512]{1,0:T(8,128)(2,1)} fusion(f32[4096,512]{1,0:T(8,128)} %fusion.51, bf16[4096,512]{1,0:T(8,128)(2,1)} %get-tuple-element.24, bf16[512,512]{1,0:T(8,128)(2,1)S(1)} %copy-done.10), kind=kOutput, calls=%fused_computation.17 | convolution fusion | flops 2151677952 | bytes 17301504 | tf_op jit(solution)/shard_map/dot_general | solution.py:85
  489.1 82.0 %all-reduce.3.cloned.1.call-done = (bf16[1,512,512]{1,2,0:T(8,128)(2,1)}, bf16[1,512,512]{1,2,0:T(8,128)(2,1)}) async-done(((bf16[1,512,512]{1,2,0:T(8,128)(2,1)}, bf16[1,512,512]{1,2,0:T(8,128)(2,1)}), (bf16[1,512,512]{1,2,0:T(8,128)(2,1)}, bf16[1,512,512]{1,2,0:T(8,128)(2,1)})) %all-reduce.3.cloned.1.call-update) | async-done | bytes 1048592 | tf_op jit(solution)/shard_map/psum | solution.py:93
  571.1 1.3 maximum_convert_fusion
  572.4 1.8 copy.135
  (16 shorter events, 0.0 us)
Async XLA Ops:
  7.2 21.3 %copy-start = (bf16[512,512]{1,0:T(8,128)(2,1)S(1)}, bf16[512,512]{1,0:T(8,128)(2,1)}, u32[]{:S(2)}) copy-start(bf16[512,512]{1,0:T(8,128)(2,1)} %param.11) | copy-start | bytes 1572868
  7.2 8.0 %copy-start.9 = (bf16[256,256]{1,0:T(8,128)(2,1)S(1)}, bf16[256,256]{1,0:T(8,128)(2,1)}, u32[]{:S(2)}) copy-start(bf16[256,256]{1,0:T(8,128)(2,1)} %param.16) | copy-start | bytes 393220
  13.2 2.0 copy-start.4
  20.9 85.0 %all-to-all-start = ((bf16[512,16,256]{2,1,0:T(8,128)(2,1)}), bf16[512,16,256]{2,1,0:T(8,128)(2,1)}, u32[]{:S(2)}, u32[]{:S(2)}) async-start(bf16[512,16,256]{2,1,0:T(8,128)(2,1)} %copy.104), calls=%async_computation | async-start | bytes 8388608 | tf_op jit(solution)/shard_map/all_to_all | solution.py:68
  28.4 6.6 %copy-start.8 = (bf16[256,256]{1,0:T(8,128)(2,1)S(1)}, bf16[256,256]{1,0:T(8,128)(2,1)}, u32[]{:S(2)}) copy-start(bf16[256,256]{1,0:T(8,128)(2,1)} %param.13) | copy-start | bytes 393220
  33.0 2.0 copy-start.5
  106.0 97.2 %all-to-all-start.2 = ((bf16[512,16,256]{2,1,0:T(8,128)(2,1)}), bf16[512,16,256]{2,1,0:T(8,128)(2,1)}, u32[]{:S(2)}, u32[]{:S(2)}) async-start(bf16[512,16,256]{2,1,0:T(8,128)(2,1)} %copy.128), calls=%async_computation.2 | async-start | bytes 8388608 | tf_op jit(solution)/shard_map/all_to_all | solution.py:43
  132.1 2.8 copy-start.7
  134.9 2.2 copy-start.2
  134.9 2.2 copy-start.6
  137.1 3.2 copy-start.1
  203.2 97.2 %all-to-all-start.1 = ((bf16[16,32,1,16,256]{4,3,1,2,0:T(8,128)(2,1)}), bf16[16,32,1,16,256]{4,3,1,2,0:T(8,128)(2,1)}, u32[]{:S(2)}, u32[]{:S(2)}) async-start(bf16[16,32,1,16,256]{4,3,1,2,0:T(8,128)(2,1)} %fusion.23), calls=%async_computation.1 | async-start | bytes 8388608 | tf_op jit(solution)/shard_map/all_to_all | solution.py:14
  225.7 6.8 %copy-start.3 = (bf16[32,256,256]{1,2,0:T(8,128)(2,1)S(1)}, bf16[32,256,256]{1,2,0:T(8,128)(2,1)}, u32[]{:S(2)}) copy-start(bf16[32,256,256]{1,2,0:T(8,128)(2,1)} %copy.107) | copy-start | bytes 12582916
  300.5 97.2 %all-to-all-start.3 = ((bf16[32,16,16,256]{3,2,0,1:T(8,128)(2,1)}), bf16[32,16,16,256]{3,2,0,1:T(8,128)(2,1)}, u32[]{:S(2)}, u32[]{:S(2)}) async-start(bf16[32,16,16,256]{3,2,0,1:T(8,128)(2,1)} %copy.132), calls=%async_computation.3 | async-start | bytes 8388608 | tf_op jit(solution)/shard_map/all_to_all | solution.py:54
  320.2 250.9 %all-reduce.3.cloned.1.call-start = ((), (), s32[]{:S(2)}) async-start(), calls=%async_computation.4 | async-start | bytes 2097152 | tf_op jit(solution)/shard_map/psum | solution.py:93
  401.4 1.3 copy-start.11
  473.2 6.7 %copy-start.10 = (bf16[512,512]{1,0:T(8,128)(2,1)S(1)}, bf16[512,512]{1,0:T(8,128)(2,1)}, u32[]{:S(2)}) copy-start(bf16[512,512]{1,0:T(8,128)(2,1)} %param.12) | copy-start | bytes 1572868
Sparse Core Ops, SparseCore 0:
  480.0 91.0 all-reduce.2
